TPU v7x, 512 devices: a whole 4x8x8 slice. The times are simulated.
512 devices in a mesh: req: 128 (over z, y, core), tp: 4 (over x).
Axes of the slice: x: 4, y: 8, z: 8, core: 2. Of those that a mesh axis runs over, the one named last changes fastest.
Arguments:
- queries: bfloat16 [49152, 2048], P('req', 'tp'), may hold values from -32 to 32
- tree_kv: bfloat16 [49152, 256], P('req'), may hold values from -6 to 6
- suffix_kv: bfloat16 [768, 256, 256], P('req'), may hold values from -6 to 6
- suffix_len: int32 [768], P('req'), may hold values from 1 to 256
- group_ids: int32 [768], P('req'), may hold values from 0 to 1
- parents: int32 [768, 64], P('req'), may hold values from 0 to 62, as said below
- accepted: int32 [768, 8], P('req'), may hold values from 0 to 63, as said below
- prompt_kv: bfloat16 [2, 4096, 256], P(None, 'req'), may hold values from -12 to 12
- out_weight: bfloat16 [2048, 2048], P('tp'), may hold values from -0.5 to 0.5
Outputs:
- layer_output: bfloat16 [49152, 2048], P(('req', 'tp'))
- path_cache: bfloat16 [768, 8, 256], P('req')
Inputs may be any that keep to these rules, and one draw needn't show every extreme that they name: parents[r, 0] = 0 and parents[r, i] < i for i >= 1, so node 0 is every tree's root. accepted[r] runs from the root down one branch: accepted[r, 0] = 0 and accepted[r, t - 1] = parents[r, accepted[r, t]].
All inputs are finite; a program needn't handle non-finite values.
Results may differ from a plain program's by a relative error of at most 0.017.
Values may be sent and summed in bfloat16 or wider, within the bound.
A program may use at most 64 MiB of HBM per device.

v0:
```python
import jax
import jax.numpy as jnp
from jax import lax
from jax.sharding import PartitionSpec as P

neg_large = -1e30
block_len = 512


def ancestry(parents):
    node_count = parents.shape[1]
    positions = jnp.arange(node_count, dtype=jnp.int32)
    step_up = (parents[:, :, None] == positions[None, None, :]) & (positions[None, :, None] > 0)
    closure = (
        jnp.where(step_up, 1.0, 0.0).astype(jnp.float32)
        + jnp.eye(node_count, dtype=jnp.float32)[None]
    )
    for repeat in range(max(1, (node_count - 1).bit_length())):
        closure = jnp.minimum(
            closure + jnp.einsum("rij,rjk->rik", closure, closure, precision=lax.Precision.HIGHEST),
            1.0,
        )
    return closure > 0.5


def absorb(softmax_state, grouped, keys_vals, valid):
    running_max, denominator, weighted = softmax_state
    head_size = grouped.shape[-1]
    scores = jnp.einsum(
        "rthd,rnd->rthn", grouped, keys_vals[..., :head_size], preferred_element_type=jnp.float32
    ) * head_size ** (-0.5)
    if valid is not None:
        scores = jnp.where(valid[:, :, None, :], scores, neg_large)
    new_max = jnp.maximum(running_max, jnp.max(scores, axis=-1))
    weights = jnp.exp(scores - new_max[..., None])
    if valid is not None:
        weights = jnp.where(valid[:, :, None, :], weights, 0.0)
    factor = jnp.exp(running_max - new_max)
    denominator = denominator * factor + jnp.sum(weights, axis=-1)
    weighted = weighted * factor[..., None] + jnp.einsum(
        "rthn,rnd->rthd",
        weights.astype(jnp.bfloat16),
        keys_vals[..., head_size:],
        preferred_element_type=jnp.float32,
    )
    return (new_max, denominator, weighted)


def absorb_prompt(softmax_state, grouped, shard_kv, group_ids):
    length = shard_kv.shape[1]
    block_count = length // block_len

    def one_block(running, number):
        block_kv = lax.dynamic_slice_in_dim(shard_kv, number * block_len, block_len, 1)
        chosen = jnp.take(block_kv, group_ids, axis=0)
        return (absorb(running, grouped, chosen, None), None)

    softmax_state, unused = lax.scan(
        one_block, softmax_state, jnp.arange(block_count, dtype=jnp.int32)
    )
    return softmax_state


def local(
    queries, tree_kv, suffix_kv, suffix_len, group_ids, parents, accepted, prompt_kv, out_weight
):
    requests, node_count = parents.shape
    pair_width = tree_kv.shape[1]
    head_size = pair_width // 2
    head_count = queries.shape[1] // head_size
    grouped = queries.reshape(requests, node_count, head_count, head_size)
    own_keys = tree_kv.reshape(requests, node_count, pair_width)
    start_state = (
        jnp.full((requests, node_count, head_count), neg_large, jnp.float32),
        jnp.zeros((requests, node_count, head_count), jnp.float32),
        jnp.zeros((requests, node_count, head_count, head_size), jnp.float32),
    )
    softmax_state = absorb(start_state, grouped, own_keys, ancestry(parents))
    slot_count = suffix_kv.shape[1]
    used_slots = jnp.arange(slot_count, dtype=jnp.int32)[None, None, :] < suffix_len[:, None, None]
    softmax_state = absorb(softmax_state, grouped, suffix_kv, used_slots)
    softmax_state = absorb_prompt(
        softmax_state, grouped, lax.all_gather(prompt_kv, "req", axis=1, tiled=True), group_ids
    )
    running_max, denominator, weighted = softmax_state
    attended = (
        (weighted / denominator[..., None])
        .astype(jnp.bfloat16)
        .reshape(requests * node_count, head_count * head_size)
    )
    layer_output = lax.psum_scatter(
        jnp.dot(attended, out_weight, preferred_element_type=jnp.float32).astype(jnp.bfloat16),
        "tp",
        scatter_dimension=0,
        tiled=True,
    )
    path_cache = jnp.take_along_axis(own_keys, accepted[:, :, None], axis=1)
    return (layer_output, path_cache)


def solution(mesh):
    return jax.shard_map(
        local,
        mesh=mesh,
        in_specs=(
            P("req", "tp"),
            P("req", None),
            P("req", None, None),
            P("req"),
            P("req"),
            P("req", None),
            P("req", None),
            P(None, "req", None),
            P("tp", None),
        ),
        out_specs=(P(("req", "tp"), None), P("req", None, None)),
        check_vma=False,
    )
```

profile of v0, /device:TPU:8, one launch (start us, length us, event | category | flops | bytes accessed | tf_op | source)
XLA Modules:
  0.0 208.7 jit_solution(16839389815929757451)
XLA Ops:
  7.2 0.7 all-gather.2.cloned.1.call-update
  8.0 1.2 fusion.17
  11.2 0.8 copy.14
  13.4 0.6 fusion.16
  14.0 0.9 fusion.13
  15.3 84.6 %all-gather.2.cloned.1.call-done = bf16[2,4096,256]{2,1,0:T(8,128)(2,1)} async-done(((bf16[2,32,256]{2,1,0:T(8,128)(2,1)}), bf16[2,4096,256]{2,1,0:T(8,128)(2,1)}) %all-gather.2.cloned.1.call-update) | async-done | bytes 4194320 | tf_op jit(solution)/shard_map/all_gather | solution.py:83
  100.0 70.5 %while.14 = (s32[]{:T(128)}, f32[6,64,4]{1,2,0:T(4,128)S(1)}, f32[6,64,4]{1,2,0:T(4,128)S(1)}, f32[6,64,4,128]{3,1,2,0:T(8,128)S(1)}, s32[6]{0:T(128)S(1)}, /*in...) while((s32[]{:T(128)}, f32[6,64,4]{1,2,0:T(4,128)S(1)}, ...), condition=%wide.region_7.8_spmd, body=%wide.region_4.7_spmd.sunk | while | flops 410128448 | bytes 22004052 | solution.py:58
  101.1 1.1 constant_dynamic-slice_fusion.2
  102.2 1.9 gather_fusion
  104.1 1.7 broadcast_select_fusion.2
  105.8 0.7 bitcast_reduce_fusion.2
  106.5 1.0 fusion.79
  107.5 1.2 fusion.80
  108.8 0.6 dynamic_slice.11
  109.9 1.1 constant_dynamic-slice_fusion.2
  111.1 1.9 gather_fusion
  113.0 1.7 broadcast_select_fusion.2
  114.6 0.7 bitcast_reduce_fusion.2
  115.3 1.0 fusion.79
  116.3 1.2 fusion.80
  117.6 0.6 dynamic_slice.11
  118.8 1.1 constant_dynamic-slice_fusion.2
  119.9 1.9 gather_fusion
  121.8 1.7 broadcast_select_fusion.2
  123.5 0.7 bitcast_reduce_fusion.2
  124.1 1.0 fusion.79
  125.1 1.2 fusion.80
  126.4 0.6 dynamic_slice.11
  127.6 1.1 constant_dynamic-slice_fusion.2
  128.7 1.9 gather_fusion
  130.6 1.7 broadcast_select_fusion.2
  132.3 0.7 bitcast_reduce_fusion.2
  133.0 1.0 fusion.79
  134.0 1.2 fusion.80
  136.4 1.1 constant_dynamic-slice_fusion.2
  137.5 1.9 gather_fusion
  139.4 1.7 broadcast_select_fusion.2
  141.1 0.7 bitcast_reduce_fusion.2
  141.8 1.0 fusion.79
  142.8 1.2 fusion.80
  145.2 1.1 constant_dynamic-slice_fusion.2
  146.3 1.9 gather_fusion
  148.2 1.7 broadcast_select_fusion.2
  149.9 0.7 bitcast_reduce_fusion.2
  150.6 1.0 fusion.79
  151.6 1.2 fusion.80
  152.9 0.6 dynamic_slice.11
  154.0 1.1 constant_dynamic-slice_fusion.2
  155.1 1.9 gather_fusion
  157.0 1.7 broadcast_select_fusion.2
  158.7 0.7 bitcast_reduce_fusion.2
  159.4 1.0 fusion.79
  160.4 1.2 fusion.80
  162.8 1.1 constant_dynamic-slice_fusion.2
  164.0 1.9 gather_fusion
  165.9 1.7 broadcast_select_fusion.2
  167.5 0.7 bitcast_reduce_fusion.2
  168.2 1.0 fusion.79
  169.2 1.2 fusion.80
  171.1 2.2 %convolution_convert_fusion = bf16[384,2048]{1,0:T(8,128)(2,1)} fusion(bf16[512,2048]{1,0:T(8,128)(2,1)S(1)} %copy-done, bf16[48,8,4,128]{3,2,1,0:T(4,128)(2,1)S(1)} %bitcast.122), kind=kOutput, calls=%fused_computation.24 | convolution fusion | flops 806092800 | bytes 4063232 | tf_op jit(solution)/shard_map/dot_general | solution.py:92
  173.3 0.7 copy-done.7
  174.2 1.0 gather_fusion.1
  175.2 0.7 bitcast_select_fusion
  175.9 25.9 %reduce-scatter.2.cloned.1.call-done = bf16[96,2048]{1,0:T(8,128)(2,1)} async-done(((bf16[384,2048]{1,0:T(8,128)(2,1)}), bf16[96,2048]{1,0:T(8,128)(2,1)}) %reduce-scatter.2.cloned.1.call-update) | async-done | bytes 393232 | tf_op jit(solution)/shard_map/reduce_scatter | solution.py:91
  (110 shorter events, 7.3 us)
Async XLA Ops:
  7.2 163.9 %copy-start = (bf16[512,2048]{1,0:T(8,128)(2,1)S(1)}, bf16[512,2048]{1,0:T(8,128)(2,1)}, u32[]{:S(2)}) copy-start(bf16[512,2048]{1,0:T(8,128)(2,1)} %param.19) | copy-start | bytes 6291460
  7.2 92.8 %all-gather.2.cloned.1.call-start = ((), (), s32[]{:S(2)}) async-start(), calls=%async_computation.1 | async-start | bytes 4227072 | tf_op jit(solution)/shard_map/all_gather | solution.py:83
  7.9 193.9 %reduce-scatter.2.cloned.1.call-start = ((), (), s32[]{:S(2)}) async-start(), calls=%async_computation.2 | async-start | bytes 1966080 | tf_op jit(solution)/shard_map/reduce_scatter | solution.py:91
  8.0 3.1 %copy-start.4 = (bf16[384,512]{1,0:T(8,128)(2,1)S(1)}, bf16[384,512]{1,0:T(8,128)(2,1)}, u32[]{:S(2)}) copy-start(bf16[384,512]{1,0:T(8,128)(2,1)} %param.11) | copy-start | bytes 1179652
  9.9 2.1 %copy-start.8 = (s32[6]{0:T(128)S(1)}, s32[6]{0:T(128)}, u32[]{:S(2)}) copy-start(s32[6]{0:T(128)} %param.14) | copy-start | bytes 76
  9.9 2.2 %copy-start.2 = (bf16[384,256]{1,0:T(8,128)(2,1)S(1)}, bf16[384,256]{1,0:T(8,128)(2,1)}, u32[]{:S(2)}) copy-start(bf16[384,256]{1,0:T(8,128)(2,1)} %param.12) | copy-start | bytes 589828
  11.2 1.5 copy-start.5
  13.4 1.5 copy-start.6
  14.9 85.1 %copy-start.9 = (s32[6]{0:T(128)S(1)}, s32[6]{0:T(128)}, u32[]{:S(2)}) copy-start(s32[6]{0:T(128)} %param.15) | copy-start | bytes 76
  104.1 1.7 copy-start.1
  113.0 1.7 copy-start.1
  121.8 1.7 copy-start.1
  130.6 1.7 copy-start.1
  139.4 1.7 copy-start.1
  148.2 1.7 copy-start.1
  157.0 1.7 copy-start.1
  165.9 1.7 copy-start.1
  173.3 0.7 copy-start.7
  173.3 0.9 copy-start.3
Sparse Core Ops, SparseCore 0:
  11.2 88.7 all-gather.1
  173.4 28.3 reduce-scatter.1
where the time goes:
time: 209 us
  waiting for transfers between devices  111 us (53%)
  local copies, waits for them, and re-layouts  31.9 us (15%)
  other arithmetic  23.4 us (11%)
  matrix products  22.5 us (11%)
  between operations  14.3 us (7%)
  loops' own time  5.25 us (3%)
    all_gather x1, waiting for transfers between devices, local(): lax.all_gather(prompt_kv, 'req', axis=1, tiled=True)  84.6 us
    reduce_scatter x1, waiting for transfers between devices, local(): lax.psum_scatter(jnp.dot(attended, out_weight, preferred_element_type=jnp...  25.9 us
    gather x8, local copies, waits for them, and re-layouts, one_block(): chosen = jnp.take(block_kv, group_ids, axis=0)  15.2 us
    select_n x16, other arithmetic, one_block(): chosen = jnp.take(block_kv, group_ids, axis=0)  13.4 us
    dot_general x10, matrix products, absorb(): jnp.einsum('rthn,rnd->rthd', weights.astype(jnp.bfloat16), keys_vals[...,...  11.3 us
    dynamic_slice x8, local copies, waits for them, and re-layouts, one_block(): lax.dynamic_slice_in_dim(shard_kv, number * block_len, block_len, 1)  8.68 us
    reduce_sum x10, other arithmetic, absorb(): denominator = denominator * factor + jnp.sum(weights, axis=-1)  8.67 us
    dot_general x10, matrix products, absorb(): jnp.einsum('rthd,rnd->rthn', grouped, keys_vals[..., :head_size], preferr...  6.25 us
  transfers between devices with their start and end apart: 2, of which 2 were waited for; matrix products, arithmetic and copies ran while one was open for 4% of the time, Pallas kernels for 0%

commit v1 on v0

--- a/solution.py
+++ b/solution.py
@@ -80,7 +80,12 @@
     used_slots = jnp.arange(slot_count, dtype=jnp.int32)[None, None, :] < suffix_len[:, None, None]
     softmax_state = absorb(softmax_state, grouped, suffix_kv, used_slots)
     softmax_state = absorb_prompt(
-        softmax_state, grouped, lax.all_gather(prompt_kv, "req", axis=1, tiled=True), group_ids
+        softmax_state,
+        grouped,
+        jnp.concatenate(
+            lax.all_to_all(jnp.stack([prompt_kv] * lax.axis_size("req")), "req", 0, 0), axis=1
+        ),
+        group_ids,
     )
     running_max, denominator, weighted = softmax_state
     attended = (

time: 209 us -> 245 us (1.17)
  starting transfers between devices: 0.08 us -> 18 us
  waiting for transfers between devices: 111 us -> 121 us
  local copies, waits for them, and re-layouts: 31.9 us -> 40 us
    all_to_all x0 -> x1, waiting for transfers between devices: none -> 91 us  [local(): lax.all_to_all(jnp.stack([prompt_kv] * lax.axis_size('req')), 'req', 0, 0)]
    all_gather x1 -> x0, waiting for transfers between devices: 84.6 us -> none  [local(): lax.all_gather(prompt_kv, 'req', axis=1, tiled=True)]
    all_to_all x0 -> x1, starting transfers between devices: none -> 18 us  [local(): lax.all_to_all(jnp.stack([prompt_kv] * lax.axis_size('req')), 'req', 0, 0)]
    all_to_all x0 -> x1, local copies, waits for them, and re-layouts: none -> 4.66 us  [local(): lax.all_to_all(jnp.stack([prompt_kv] * lax.axis_size('req')), 'req', 0, 0)]
    reduce_scatter x1, waiting for transfers between devices: 25.9 us -> 29.8 us  [local(): lax.psum_scatter(jnp.dot(attended, out_weight, preferred_element_type=jnp...]
    another operation x0 -> x1, local copies, waits for them, and re-layouts: none -> 3.37 us  [local(): jnp.stack([prompt_kv] * lax.axis_size('req'))]
where the time goes in v1:
time: 245 us; the launch traced here: 244 us
  waiting for transfers between devices  121 us (49%)
  local copies, waits for them, and re-layouts  40 us (16%)
  other arithmetic  23.4 us (10%)
  matrix products  22.7 us (9%)
  starting transfers between devices  18 us (7%)
  between operations  14.3 us (6%)
  loops' own time  5.25 us (2%)
    all_to_all x1, waiting for transfers between devices, local(): lax.all_to_all(jnp.stack([prompt_kv] * lax.axis_size('req')), 'req', 0, 0)  91 us
    reduce_scatter x1, waiting for transfers between devices, local(): lax.psum_scatter(jnp.dot(attended, out_weight, preferred_element_type=jnp...  29.8 us
    all_to_all x1, starting transfers between devices, local(): lax.all_to_all(jnp.stack([prompt_kv] * lax.axis_size('req')), 'req', 0, 0)  18 us
    gather x8, local copies, waits for them, and re-layouts, one_block(): chosen = jnp.take(block_kv, group_ids, axis=0)  15.2 us
    select_n x16, other arithmetic, one_block(): chosen = jnp.take(block_kv, group_ids, axis=0)  13.4 us
    dot_general x10, matrix products, absorb(): jnp.einsum('rthn,rnd->rthd', weights.astype(jnp.bfloat16), keys_vals[...,...  11.2 us
    dynamic_slice x8, local copies, waits for them, and re-layouts, one_block(): lax.dynamic_slice_in_dim(shard_kv, number * block_len, block_len, 1)  8.68 us
    reduce_sum x10, other arithmetic, absorb(): denominator = denominator * factor + jnp.sum(weights, axis=-1)  8.66 us
  transfers between devices with their start and end apart: 2, of which 2 were waited for; matrix products, arithmetic and copies ran while one was open for 4% of the time, Pallas kernels for 0%

profile of v1, /device:TPU:8, one launch (start us, length us, event | category | flops | bytes accessed | tf_op | source)
XLA Modules:
  0.0 244.4 jit_solution(13453281950461813653)
XLA Ops:
  7.2 3.4 %stack.2 = bf16[128,2,32,256]{3,2,1,0:T(8,128)(2,1)} broadcast(bf16[2,32,256]{2,1,0:T(8,128)(2,1)} %param.18), dimensions={1,2,3} | broadcast | bytes 4227072 | tf_op jit(solution)/shard_map/stack | solution.py:86
  10.6 18.0 %all-to-all-start = ((bf16[128,2,32,256]{3,2,1,0:T(8,128)(2,1)}), bf16[128,2,32,256]{3,2,1,0:T(8,128)(2,1)}, u32[]{:S(2)}, u32[]{:S(2)}) async-start(bf16[128,2,32,256]{3,2,1,0:T(8,128)(2,1)} %stack.2), calls=%async_computation | async-start | bytes 8388608 | tf_op jit(solution)/shard_map/all_to_all | solution.py:86
  31.0 0.8 copy.26
  32.5 1.5 fusion.58
  34.2 0.6 fusion.16
  34.9 0.8 fusion.13
  36.2 91.0 %all-to-all-done = bf16[128,2,32,256]{3,2,1,0:T(8,128)(2,1)} async-done(((bf16[128,2,32,256]{3,2,1,0:T(8,128)(2,1)}), bf16[128,2,32,256]{3,2,1,0:T(8,128)(2,1)}, u32[]{:S(2)}, u32[]{:S(2)}) %all-to-all-start) | async-done | bytes 4194336 | tf_op jit(solution)/shard_map/all_to_all | solution.py:86
  127.2 4.7 %copy.29 = bf16[128,2,32,256]{3,2,0,1:T(8,128)(2,1)} copy(bf16[128,2,32,256]{3,2,1,0:T(8,128)(2,1)} %all-to-all-done) | data formatting | bytes 8388608 | tf_op jit(solution)/shard_map/all_to_all | solution.py:86
  131.9 70.5 %while.14 = (s32[]{:T(128)}, f32[6,64,4]{1,2,0:T(4,128)S(1)}, f32[6,64,4]{1,2,0:T(4,128)S(1)}, f32[6,64,4,128]{3,1,2,0:T(8,128)S(1)}, s32[6]{0:T(128)S(1)}, /*in...) while((s32[]{:T(128)}, f32[6,64,4]{1,2,0:T(4,128)S(1)}, ...), condition=%wide.region_7.8_spmd, body=%wide.region_4.7_spmd.sunk | while | flops 410128448 | bytes 22004052 | solution.py:58
  133.0 1.1 constant_dynamic-slice_fusion.2
  134.2 1.9 gather_fusion
  136.1 1.7 broadcast_select_fusion.2
  137.7 0.7 bitcast_reduce_fusion.2
  138.4 1.0 fusion.79
  139.4 1.2 fusion.80
  140.7 0.6 dynamic_slice.11
  141.9 1.1 constant_dynamic-slice_fusion.2
  143.0 1.9 gather_fusion
  144.9 1.7 broadcast_select_fusion.2
  146.6 0.7 bitcast_reduce_fusion.2
  147.2 1.0 fusion.79
  148.2 1.2 fusion.80
  150.7 1.1 constant_dynamic-slice_fusion.2
  151.8 1.9 gather_fusion
  153.7 1.7 broadcast_select_fusion.2
  155.4 0.7 bitcast_reduce_fusion.2
  156.0 1.0 fusion.79
  157.0 1.2 fusion.80
  158.3 0.6 dynamic_slice.11
  159.5 1.1 constant_dynamic-slice_fusion.2
  160.6 1.9 gather_fusion
  162.5 1.7 broadcast_select_fusion.2
  164.2 0.7 bitcast_reduce_fusion.2
  164.9 1.0 fusion.79
  165.9 1.2 fusion.80
  168.3 1.1 constant_dynamic-slice_fusion.2
  169.4 1.9 gather_fusion
  171.3 1.7 broadcast_select_fusion.2
  173.0 0.7 bitcast_reduce_fusion.2
  173.7 1.0 fusion.79
  174.7 1.2 fusion.80
  177.1 1.1 constant_dynamic-slice_fusion.2
  178.2 1.9 gather_fusion
  180.1 1.7 broadcast_select_fusion.2
  181.8 0.7 bitcast_reduce_fusion.2
  182.5 1.0 fusion.79
  183.5 1.2 fusion.80
  185.9 1.1 constant_dynamic-slice_fusion.2
  187.0 1.9 gather_fusion
  188.9 1.7 broadcast_select_fusion.2
  190.6 0.7 bitcast_reduce_fusion.2
  191.3 1.0 fusion.79
  192.3 1.2 fusion.80
  194.7 1.1 constant_dynamic-slice_fusion.2
  195.8 1.9 gather_fusion
  197.7 1.7 broadcast_select_fusion.2
  199.4 0.7 bitcast_reduce_fusion.2
  200.1 1.0 fusion.79
  201.1 1.2 fusion.80
  203.0 2.2 convolution_convert_fusion
  205.2 0.7 copy-done.7
  206.1 1.0 gather_fusion.1
  207.1 0.7 bitcast_select_fusion
  207.8 29.8 %reduce-scatter.2.cloned.1.call-done = bf16[96,2048]{1,0:T(8,128)(2,1)} async-done(((bf16[384,2048]{1,0:T(8,128)(2,1)}), bf16[96,2048]{1,0:T(8,128)(2,1)}) %reduce-scatter.2.cloned.1.call-update) | async-done | bytes 393232 | tf_op jit(solution)/shard_map/reduce_scatter | solution.py:96
  (113 shorter events, 8.5 us)
Async XLA Ops:
  7.2 195.8 %copy-start = (bf16[512,2048]{1,0:T(8,128)(2,1)S(1)}, bf16[512,2048]{1,0:T(8,128)(2,1)}, u32[]{:S(2)}) copy-start(bf16[512,2048]{1,0:T(8,128)(2,1)} %param.19) | copy-start | bytes 6291460
  10.5 18.0 %copy-start.9 = (s32[6,64]{1,0:T(8,128)S(1)}, s32[6,64]{1,0:T(8,128)}, u32[]{:S(2)}) copy-start(s32[6,64]{1,0:T(8,128)} %param.16) | copy-start | bytes 4612
  10.6 116.7 %all-to-all-start = ((bf16[128,2,32,256]{3,2,1,0:T(8,128)(2,1)}), bf16[128,2,32,256]{3,2,1,0:T(8,128)(2,1)}, u32[]{:S(2)}, u32[]{:S(2)}) async-start(bf16[128,2,32,256]{3,2,1,0:T(8,128)(2,1)} %stack.2), calls=%async_computation | async-start | bytes 8388608 | tf_op jit(solution)/shard_map/all_to_all | solution.py:86
  28.5 209.0 %reduce-scatter.2.cloned.1.call-start = ((), (), s32[]{:S(2)}) async-start(), calls=%async_computation.2 | async-start | bytes 1966080 | tf_op jit(solution)/shard_map/reduce_scatter | solution.py:96
  28.6 2.3 copy-start.5
  29.8 2.1 copy-start.8
  29.8 2.2 copy-start.2
  33.9 0.9 copy-start.3
  34.2 1.5 copy-start.6
  36.2 95.7 %copy-start.10 = (s32[6]{0:T(128)S(1)}, s32[6]{0:T(128)}, u32[]{:S(2)}) copy-start(s32[6]{0:T(128)} %param.15) | copy-start | bytes 76
  136.1 1.7 copy-start.1
  144.9 1.7 copy-start.1
  153.7 1.7 copy-start.1
  162.5 1.7 copy-start.1
  171.3 1.7 copy-start.1
  180.1 1.7 copy-start.1
  188.9 1.7 copy-start.1
  197.7 1.7 copy-start.1
  205.1 0.7 copy-start.7
  205.1 0.9 copy-start.4
Sparse Core Ops, SparseCore 0:
  205.3 32.2 reduce-scatter.1
